TPU v7x, 256 devices: a whole 4x4x8 slice. The times are simulated.
256 devices in a mesh: clus: 32 (over y, z), tgt: 8 (over x, core).
Axes of the slice: x: 4, y: 4, z: 8, core: 2. Of those that a mesh axis runs over, the one named last changes fastest.
Arguments:
- weights_init: float32 [262144, 1024], P('clus', 'tgt'), may hold values from -6 to 6
- margins: float32 [4096, 1024], P('clus', 'tgt')
- block_bits: int32 [9216, 128, 8], P('clus'), may hold values from 0 to 65535
- block_run_index: int32 [9216], P('clus'), may hold values from 0 to 31, as said below
- block_col: int32 [9216], P('clus'), may hold values from 0 to 63
- block_tally: int32 [32], P('clus'), may hold values from 144 to 288, as said below
- step_size: float32 [1], replicated, may hold values from 0.3 to 0.6
- penalty: float32 [1], replicated, may hold values from 0.3 to 0.8
Outputs:
- weights: float32 [262144, 1024], P('clus', 'tgt')
- run_loss: float32 [4096], P('clus')
Inputs may be any that keep to these rules, and one draw needn't show every extreme that they name: `block_run_index`: A device's slots name distinct pairs of run block and cluster block. `block_tally`: some device's list is full in every draw.
All inputs are finite; a program needn't handle non-finite values.
Results may differ from a plain program's by a relative error of at most 0.0025.
Values may be sent and summed in bfloat16 or wider, within the bound.
No kernel may reach another device: no remote copies, remote signals or barrier semaphores. Data moves between devices by JAX's collectives and lax.ppermute only.
A program may use at most 128 MiB of HBM per device.

v0:
```python
import math
import jax
import jax.numpy as jnp
from jax import lax
from jax.sharding import PartitionSpec as P

BLOCK_ENTRIES = 128
TARGETS = 1024
ITERS = 2


def pick_blocks(index, count, table):
    selector = (index[:, None] == jnp.arange(count, dtype=jnp.int32)[None, :]).astype(table.dtype)
    flat = table.reshape(count, -1)
    picked = jnp.dot(selector, flat, preferred_element_type=jnp.float32).astype(table.dtype)
    return picked.reshape((index.shape[0],) + table.shape[1:])


def add_blocks(total, index, values):
    count = total.shape[0]
    selector = (jnp.arange(count, dtype=jnp.int32)[:, None] == index[None, :]).astype(jnp.float32)
    flat = values.reshape(index.shape[0], -1)
    summed = jnp.dot(
        selector, flat, preferred_element_type=jnp.float32, precision=lax.Precision.HIGHEST
    )
    return total + summed.reshape(total.shape)


def per_device(
    weights_init, margins, block_bits, block_run_index, block_col, block_tally, step_size, penalty
):
    slot_total = block_run_index.shape[0]
    nblocks = weights_init.shape[0] // BLOCK_ENTRIES
    tcols = weights_init.shape[1]
    ndev = lax.axis_size("clus")
    group_index = math.gcd(slot_total, 36)
    rotation_turns = slot_total // group_index
    live_slots = (jnp.arange(slot_total, dtype=jnp.int32) < block_tally[0]).astype(jnp.bfloat16)
    shifts = jnp.arange(16, dtype=jnp.int32)
    packed_flags = jnp.right_shift(block_bits[..., None], shifts) & 1
    sign_values = (2 * packed_flags - 1).astype(jnp.bfloat16).reshape(
        slot_total, BLOCK_ENTRIES, BLOCK_ENTRIES
    ) * live_slots[:, None, None]
    sign_groups = sign_values.reshape(rotation_turns, group_index, BLOCK_ENTRIES, BLOCK_ENTRIES)
    place_groups = block_run_index.reshape(rotation_turns, group_index)
    col_groups = block_col.reshape(rotation_turns, group_index)
    eta = step_size[0]
    thresh = eta * penalty[0]
    current = weights_init
    err = jnp.zeros((BLOCK_ENTRIES, tcols), jnp.float32)
    for step in range(ITERS):
        current_b = current.astype(jnp.bfloat16).reshape(nblocks, BLOCK_ENTRIES, tcols)

        def forward(total, portion):
            scan_inputs, pos, cols = portion
            selected_block = pick_blocks(cols, nblocks, current_b)
            product_rows = jnp.einsum(
                "vjs,vsh->vjh", scan_inputs, selected_block, preferred_element_type=jnp.float32
            )
            return (add_blocks(total, pos, product_rows), None)

        total, unused = lax.scan(
            forward,
            jnp.zeros((ndev, BLOCK_ENTRIES, tcols), jnp.float32),
            (sign_groups, place_groups, col_groups),
        )
        owned = lax.psum_scatter(
            total.reshape(ndev * BLOCK_ENTRIES, tcols).astype(jnp.bfloat16),
            "clus",
            scatter_dimension=0,
            tiled=True,
        ).astype(jnp.float32)
        err = owned / 128.0 - margins
        err_b = err.astype(jnp.bfloat16)
        residual_table = lax.all_gather(err_b, "clus", axis=0, tiled=True).reshape(
            ndev, BLOCK_ENTRIES, tcols
        )

        def backward(total, portion):
            scan_inputs, pos, cols = portion
            design_rows = pick_blocks(pos, ndev, residual_table)
            part = jnp.einsum(
                "oeq,oei->oqi", scan_inputs, design_rows, preferred_element_type=jnp.float32
            )
            return (add_blocks(total, cols, part), None)

        grads, unused = lax.scan(
            backward,
            jnp.zeros((nblocks, BLOCK_ENTRIES, tcols), jnp.float32),
            (sign_groups, place_groups, col_groups),
        )
        grad = grads.reshape(nblocks * BLOCK_ENTRIES, tcols) / 128.0
        moved = current - eta * grad
        current = jnp.sign(moved) * jnp.maximum(jnp.abs(moved) - thresh, 0.0)
    squares = jnp.sum(err * err, axis=1)
    run_loss = lax.psum(squares, "tgt") / TARGETS
    return (current, run_loss)


def solution(mesh):
    return jax.shard_map(
        per_device,
        mesh=mesh,
        in_specs=(
            P("clus", "tgt"),
            P("clus", "tgt"),
            P("clus", None, None),
            P("clus"),
            P("clus"),
            P("clus"),
            P(),
            P(),
        ),
        out_specs=(P("clus", "tgt"), P("clus")),
        check_vma=False,
    )
```

profile of v0, /device:TPU:2, one launch (start us, length us, event | category | flops | bytes accessed | tf_op | source)
XLA Modules:
  0.0 1006.4 jit_solution(12187850462215080191)
XLA Ops:
  8.0 9.2 shift_right_arithmetic.21
  17.2 14.9 %fusion.60 = bf16[8,36,128,128]{2,3,1,0:T(8,128)(2,1)} fusion(s32[8,36,128,128]{2,3,1,0:T(8,128)} %bitcast.215, s32[128]{0:T(128)S(1)} %shift_right_arithmetic.24, bf16[8,36]{1,0:T(8,128)(2,1)S(1)} %fusion.63), kind=kLoop, calls=%fused_computation.77 | loop fusion | flops 42467328 | bytes 28312640 | tf_op jit(solution)/shard_map/mul | solution.py:41
  32.1 12.7 %copy.20 = bf16[8,36,128,128]{3,2,1,0:T(8,128)(2,1)} copy(bf16[8,36,128,128]{2,3,1,0:T(8,128)(2,1)} %fusion.60) | data formatting | bytes 18874368
  50.0 80.1 %while.48 = (s32[]{:T(128)}, f32[32,128,128]{2,0,1:T(8,128)}, s32[8,36]{1,0:T(8,128)S(1)}, bf16[8,36,128,128]{3,2,1,0:T(8,128)(2,1)}, s32[8,36]{1,0:T(8,128)S(1)...) while((s32[]{:T(128)}, f32[32,128,128]{2,0,1:T(8,128)}, ...), condition=%wide.wide.region_1.2_spmd.clone, body=%wide.wide.region_0.1_spmd.clone.sunk | while | flops 454626688 | bytes 21890508 | solution.py:62
  133.5 220.0 %reduce-scatter.3.cloned.1.call-done = bf16[128,128]{1,0:T(8,128)(2,1)} async-done(((bf16[4096,128]{1,0:T(8,128)(2,1)}), bf16[128,128]{1,0:T(8,128)(2,1)}) %reduce-scatter.3.cloned.1.call-update) | async-done | bytes 32784 | tf_op jit(solution)/shard_map/reduce_scatter | solution.py:67
  356.4 74.3 %all-gather.3.cloned.1.call-done = bf16[4096,128]{1,0:T(8,128)(2,1)} async-done(((bf16[128,128]{1,0:T(8,128)(2,1)}), bf16[4096,128]{1,0:T(8,128)(2,1)}) %all-gather.3.cloned.1.call-update) | async-done | bytes 1048592 | tf_op jit(solution)/shard_map/all_gather | solution.py:75
  432.3 83.9 %while.49 = (s32[]{:T(128)}, f32[64,128,128]{2,0,1:T(8,128)}, s32[8,36]{1,0:T(8,128)S(1)}, bf16[8,36,128,128]{2,3,1,0:T(8,128)(2,1)}, s32[8,36]{1,0:T(8,128)S(1)...) while((s32[]{:T(128)}, f32[64,128,128]{2,0,1:T(8,128)}, ...), condition=%wide.wide.region_4.5_spmd.clone, body=%wide.wide.region_3.4_spmd.clone.sunk | while | flops 644418944 | bytes 25036236 | solution.py:87
  443.8 7.9 select_add_fusion.13
  465.3 7.9 select_add_fusion.13
  476.1 7.9 select_add_fusion.13
  486.8 7.9 select_add_fusion.13
  508.3 7.9 select_add_fusion.13
  527.9 80.0 %while.50 = (s32[]{:T(128)}, f32[32,128,128]{2,0,1:T(8,128)}, s32[8,36]{1,0:T(8,128)S(1)}, bf16[8,36,128,128]{3,2,1,0:T(8,128)(2,1)}, s32[8,36]{1,0:T(8,128)S(1)...) while((s32[]{:T(128)}, f32[32,128,128]{2,0,1:T(8,128)}, ...), condition=%wide.wide.region_6.7_spmd.clone, body=%wide.wide.region_5.6_spmd.clone.sunk | while | flops 454626688 | bytes 21890508 | solution.py:62
  611.2 214.7 %reduce-scatter.5.cloned.1.call-done = bf16[128,128]{1,0:T(8,128)(2,1)} async-done(((bf16[4096,128]{1,0:T(8,128)(2,1)}), bf16[128,128]{1,0:T(8,128)(2,1)}) %reduce-scatter.5.cloned.1.call-update) | async-done | bytes 32784 | tf_op jit(solution)/shard_map/reduce_scatter | solution.py:67
  827.3 10.2 %psum.7 = f32[128]{0:T(128)S(1)} all-reduce(f32[128]{0:T(128)S(1)} %get-tuple-element.298), channel_id=1, replica_groups=mesh['clus'=32,'tgt'=8] {'tgt'}, use_global_device_ids=true, to_apply=%region_11.12 | all-reduce | flops 128 | bytes 1024 | tf_op jit(solution)/shard_map/psum | solution.py:96
  838.0 65.1 %all-gather.5.cloned.1.call-done = bf16[4096,128]{1,0:T(8,128)(2,1)} async-done(((bf16[128,128]{1,0:T(8,128)(2,1)}), bf16[4096,128]{1,0:T(8,128)(2,1)}) %all-gather.5.cloned.1.call-update) | async-done | bytes 1048592 | tf_op jit(solution)/shard_map/all_gather | solution.py:75
  904.6 83.9 %while.51 = (s32[]{:T(128)}, f32[64,128,128]{2,0,1:T(8,128)}, s32[8,36]{1,0:T(8,128)S(1)}, bf16[8,36,128,128]{2,3,1,0:T(8,128)(2,1)}, s32[8,36]{1,0:T(8,128)S(1)...) while((s32[]{:T(128)}, f32[64,128,128]{2,0,1:T(8,128)}, ...), condition=%wide.wide.region_9.10_spmd.clone, body=%wide.wide.region_8.9_spmd.clone.sunk | while | flops 644418944 | bytes 25036236 | solution.py:87
  916.1 7.9 select_add_fusion.15
  926.8 7.9 select_add_fusion.15
  937.6 7.9 select_add_fusion.15
  948.4 7.9 select_add_fusion.15
  959.1 7.9 select_add_fusion.15
  969.9 7.9 select_add_fusion.15
  980.6 7.9 select_add_fusion.15
  (233 shorter events, 273.6 us)
Async XLA Ops:
  7.2 346.3 %reduce-scatter.3.cloned.1.call-start = ((), (), s32[]{:S(2)}) async-start(), calls=%async_computation.2 | async-start | bytes 1081344 | tf_op jit(solution)/shard_map/reduce_scatter | solution.py:67
  32.1 12.7 %copy-start.7 = (s32[288]{0:T(512)S(1)}, s32[288]{0:T(512)}, u32[]{:S(2)}) copy-start(s32[288]{0:T(512)} %param.20) | copy-start | bytes 3460
  32.1 12.8 %copy-start.8 = (s32[288]{0:T(512)S(1)}, s32[288]{0:T(512)}, u32[]{:S(2)}) copy-start(s32[288]{0:T(512)} %param.19) | copy-start | bytes 3460
  47.4 2.7 copy-start.4
  130.2 223.3 %copy-start.6 = (f32[128,128]{1,0:T(8,128)S(1)}, f32[128,128]{1,0:T(8,128)}, u32[]{:S(2)}) copy-start(f32[128,128]{1,0:T(8,128)} %param.17) | copy-start | bytes 196612
  133.4 297.4 %all-gather.3.cloned.1.call-start = ((), (), s32[]{:S(2)}) async-start(), calls=%async_computation.3 | async-start | bytes 1081344 | tf_op jit(solution)/shard_map/all_gather | solution.py:75
  354.9 471.0 %reduce-scatter.5.cloned.1.call-start = ((), (), s32[]{:S(2)}) async-start(), calls=%async_computation.4 | async-start | bytes 1081344 | tf_op jit(solution)/shard_map/reduce_scatter | solution.py:67
  518.9 4.6 copy-start
  521.3 2.1 copy-start.2
  525.2 2.7 copy-start.5
  611.1 292.0 %all-gather.5.cloned.1.call-start = ((), (), s32[]{:S(2)}) async-start(), calls=%async_computation.5 | async-start | bytes 1081344 | tf_op jit(solution)/shard_map/all_gather | solution.py:75
  991.2 2.5 copy-start.1
  991.2 3.5 copy-start.3
Sparse Core Ops, SparseCore 0:
  133.5 219.8 reduce-scatter.2
  356.1 74.6 all-gather.2
  611.2 214.5 reduce-scatter.4
  828.3 74.7 all-gather.4
where the time goes:
time: 1010 us
  waiting for transfers between devices  574 us (57%)
  matrix products  309 us (31%)
  local copies, waits for them, and re-layouts  59.1 us (6%)
  other arithmetic  36.5 us (4%)
  between operations  15.9 us (2%)
  blocking collectives  10.2 us (1%)
    reduce_scatter x2, waiting for transfers between devices, per_device(): lax.psum_scatter(total.reshape(ndev * BLOCK_ENTRIES, tcols).astype(jnp.bf...  435 us
    dot_general x32, matrix products, add_blocks(): jnp.dot(selector, flat, preferred_element_type=jnp.float32, precision=lax...  211 us
    all_gather x2, waiting for transfers between devices, per_device(): lax.all_gather(err_b, 'clus', axis=0, tiled=True)  139 us
    dot_general x32, matrix products, pick_blocks(): jnp.dot(selector, flat, preferred_element_type=jnp.float32)  43 us
    dot_general x16, matrix products, forward(): jnp.einsum('vjs,vsh->vjh', scan_inputs, selected_block, preferred_element...  27.8 us
    dot_general x16, matrix products, backward(): jnp.einsum('oeq,oei->oqi', scan_inputs, design_rows, preferred_element_ty...  27.8 us
  transfers between devices with their start and end apart: 4, of which 4 were waited for; matrix products, arithmetic and copies ran while one was open for 0% of the time, Pallas kernels for 0%

commit v1 on v0

--- a/solution.py
+++ b/solution.py
@@ -7,6 +7,11 @@
 BLOCK_ENTRIES = 128
 TARGETS = 1024
 ITERS = 2
+
+
+def gather_over(x, axis, dim):
+    sent = jnp.stack([x] * lax.axis_size(axis))
+    return jnp.concatenate(lax.all_to_all(sent, axis, 0, 0), axis=dim)
 
 
 def pick_blocks(index, count, table):
@@ -72,9 +77,7 @@
         ).astype(jnp.float32)
         err = owned / 128.0 - margins
         err_b = err.astype(jnp.bfloat16)
-        residual_table = lax.all_gather(err_b, "clus", axis=0, tiled=True).reshape(
-            ndev, BLOCK_ENTRIES, tcols
-        )
+        residual_table = gather_over(err_b, "clus", 0).reshape(ndev, BLOCK_ENTRIES, tcols)
 
         def backward(total, portion):
             scan_inputs, pos, cols = portion

time: 1010 us -> 928 us (0.919)
  waiting for transfers between devices: 574 us -> 456 us
  starting transfers between devices: 0.34 us -> 25 us
    all_gather x2 -> x0, waiting for transfers between devices: 139 us -> none  [per_device(): lax.all_gather(err_b, 'clus', axis=0, tiled=True)]
    all_to_all x0 -> x2, waiting for transfers between devices: none -> 21.3 us  [gather_over(): return jnp.concatenate(lax.all_to_all(sent, axis, 0, 0), axis=dim)]
    all_to_all x0 -> x2, starting transfers between devices: none -> 13.6 us  [gather_over(): return jnp.concatenate(lax.all_to_all(sent, axis, 0, 0), axis=dim)]
    reduce_scatter x2, starting transfers between devices: 0.26 us -> 11.4 us  [per_device(): lax.psum_scatter(total.reshape(ndev * BLOCK_ENTRIES, tcols).astype(jnp.bf...]
where the time goes in v1:
time: 928 us; the launch traced here: 917 us
  waiting for transfers between devices  456 us (49%)
  matrix products  312 us (34%)
  local copies, waits for them, and re-layouts  63.4 us (7%)
  other arithmetic  31.7 us (3%)
  starting transfers between devices  25 us (3%)
  between operations  16.5 us (2%)
  blocking collectives  10.8 us (1%)
    reduce_scatter x2, waiting for transfers between devices, per_device(): lax.psum_scatter(total.reshape(ndev * BLOCK_ENTRIES, tcols).astype(jnp.bf...  435 us
    dot_general x32, matrix products, add_blocks(): jnp.dot(selector, flat, preferred_element_type=jnp.float32, precision=lax...  210 us
    dot_general x32, matrix products, pick_blocks(): jnp.dot(selector, flat, preferred_element_type=jnp.float32)  46.4 us
    dot_general x16, matrix products, forward(): jnp.einsum('vjs,vsh->vjh', scan_inputs, selected_block, preferred_element...  27.8 us
    dot_general x16, matrix products, backward(): jnp.einsum('oeq,oei->oqi', scan_inputs, design_rows, preferred_element_ty...  27.8 us
    all_to_all x2, waiting for transfers between devices, gather_over(): return jnp.concatenate(lax.all_to_all(sent, axis, 0, 0), axis=dim)  21.3 us
  transfers between devices with their start and end apart: 4, of which 4 were waited for; matrix products, arithmetic and copies ran while one was open for 0% of the time, Pallas kernels for 0%

profile of v1, /device:TPU:2, one launch (start us, length us, event | category | flops | bytes accessed | tf_op | source)
XLA Modules:
  0.0 916.8 jit_solution(12318478303862591857)
XLA Ops:
  8.0 9.2 %shift_right_arithmetic.21 = s32[288,128,8,16]{1,3,2,0:T(8,128)} broadcast(s32[288,128,8]{1,2,0:T(8,128)} %param.18), dimensions={0,1,2} | broadcast | bytes 20054016 | tf_op jit(solution)/shard_map/shift_right_arithmetic | solution.py:45
  17.2 14.9 %fusion.64 = bf16[8,36,128,128]{2,3,1,0:T(8,128)(2,1)} fusion(s32[8,36,128,128]{2,3,1,0:T(8,128)} %bitcast.211, s32[128]{0:T(128)S(1)} %shift_right_arithmetic.24, bf16[8,36]{1,0:T(8,128)(2,1)S(1)} %fusion.67), kind=kLoop, calls=%fused_computation.81 | loop fusion | flops 42467328 | bytes 28312640 | tf_op jit(solution)/shard_map/mul | solution.py:46
  32.1 12.7 %copy.18 = bf16[8,36,128,128]{3,2,1,0:T(8,128)(2,1)} copy(bf16[8,36,128,128]{2,3,1,0:T(8,128)(2,1)} %fusion.64) | data formatting | bytes 18874368
  50.0 80.1 %while.48 = (s32[]{:T(128)}, f32[32,128,128]{2,0,1:T(8,128)}, s32[8,36]{1,0:T(8,128)S(1)}, bf16[8,36,128,128]{3,2,1,0:T(8,128)(2,1)}, s32[8,36]{1,0:T(8,128)S(1)...) while((s32[]{:T(128)}, f32[32,128,128]{2,0,1:T(8,128)}, ...), condition=%wide.wide.region_1.2_spmd.clone, body=%wide.wide.region_0.1_spmd.clone.sunk | while | flops 454626688 | bytes 21890508 | solution.py:67
  134.0 220.1 %reduce-scatter.3.cloned.1.call-done = bf16[128,128]{1,0:T(8,128)(2,1)} async-done(((bf16[4096,128]{1,0:T(8,128)(2,1)}), bf16[128,128]{1,0:T(8,128)(2,1)}) %reduce-scatter.3.cloned.1.call-update) | async-done | bytes 32784 | tf_op jit(solution)/shard_map/reduce_scatter | solution.py:72
  362.9 11.4 %reduce-scatter.5.cloned.1.call-start = ((), (), s32[]{:S(2)}) async-start(), calls=%async_computation.5 | async-start | bytes 1081344 | tf_op jit(solution)/shard_map/reduce_scatter | solution.py:72
  375.6 9.8 %all-to-all-done = bf16[32,128,128]{2,1,0:T(8,128)(2,1)S(1)} async-done(((bf16[32,128,128]{2,1,0:T(8,128)(2,1)}), bf16[32,128,128]{2,1,0:T(8,128)(2,1)S(1)}, u32[]{:S(2)}, u32[]{:S(2)}) %all-to-all-start) | async-done | bytes 1048608 | tf_op jit(solution)/shard_map/all_to_all | solution.py:14
  385.4 85.6 %while.46 = (s32[]{:T(128)}, f32[64,128,128]{2,0,1:T(8,128)}, s32[8,36]{1,0:T(8,128)S(1)}, bf16[8,36,128,128]{2,3,1,0:T(8,128)(2,1)}, s32[8,36]{1,0:T(8,128)S(1)...) while((s32[]{:T(128)}, f32[64,128,128]{2,0,1:T(8,128)}, s32[8,36]{1,0:T(8,128)S(1)}, ...), condition=%wide.region_4.5_spmd.clone, body=%wide.region_3.4_spmd.clone.sunk | while | flops 644418944 | bytes 25036228 | solution.py:90
  397.3 7.9 select_add_fusion.10
  408.2 7.9 select_add_fusion.10
  419.2 7.9 select_add_fusion.10
  430.2 7.9 select_add_fusion.10
  441.2 7.9 select_add_fusion.10
  452.1 7.9 select_add_fusion.10
  482.6 79.9 %while.49 = (s32[]{:T(128)}, f32[32,128,128]{2,0,1:T(8,128)}, s32[8,36]{1,0:T(8,128)S(1)}, bf16[8,36,128,128]{3,2,1,0:T(8,128)(2,1)}, s32[8,36]{1,0:T(8,128)S(1)...) while((s32[]{:T(128)}, f32[32,128,128]{2,0,1:T(8,128)}, ...), condition=%wide.wide.region_6.7_spmd.clone, body=%wide.wide.region_5.6_spmd.clone.sunk | while | flops 454626688 | bytes 21890508 | solution.py:67
  566.3 214.8 %reduce-scatter.5.cloned.1.call-done = bf16[128,128]{1,0:T(8,128)(2,1)} async-done(((bf16[4096,128]{1,0:T(8,128)(2,1)}), bf16[128,128]{1,0:T(8,128)(2,1)}) %reduce-scatter.5.cloned.1.call-update) | async-done | bytes 32784 | tf_op jit(solution)/shard_map/reduce_scatter | solution.py:72
  789.9 10.8 %psum.7 = f32[128]{0:T(128)S(1)} all-reduce(f32[128]{0:T(128)S(1)} %get-tuple-element.298), channel_id=1, replica_groups=mesh['clus'=32,'tgt'=8] {'tgt'}, use_global_device_ids=true, to_apply=%region_11.12 | all-reduce | flops 128 | bytes 1024 | tf_op jit(solution)/shard_map/psum | solution.py:99
  801.2 11.5 %all-to-all-done.1 = bf16[32,128,128]{2,1,0:T(8,128)(2,1)S(1)} async-done(((bf16[32,128,128]{2,1,0:T(8,128)(2,1)}), bf16[32,128,128]{2,1,0:T(8,128)(2,1)S(1)}, u32[]{:S(2)}, u32[]{:S(2)}) %all-to-all-start.1) | async-done | bytes 1048608 | tf_op jit(solution)/shard_map/all_to_all | solution.py:14
  812.7 85.6 %while.47 = (s32[]{:T(128)}, f32[64,128,128]{2,0,1:T(8,128)}, s32[8,36]{1,0:T(8,128)S(1)}, bf16[8,36,128,128]{2,3,1,0:T(8,128)(2,1)}, s32[8,36]{1,0:T(8,128)S(1)...) while((s32[]{:T(128)}, f32[64,128,128]{2,0,1:T(8,128)}, s32[8,36]{1,0:T(8,128)S(1)}, ...), condition=%wide.region_9.10_spmd.clone, body=%wide.region_8.9_spmd.clone.sunk | while | flops 644418944 | bytes 25036228 | solution.py:90
  835.5 7.9 select_add_fusion.11
  846.5 7.9 select_add_fusion.11
  868.5 7.9 select_add_fusion.11
  879.4 7.9 select_add_fusion.11
  890.4 7.9 select_add_fusion.11
  (229 shorter events, 297.5 us)
Async XLA Ops:
  7.2 346.9 %reduce-scatter.3.cloned.1.call-start = ((), (), s32[]{:S(2)}) async-start(), calls=%async_computation.4 | async-start | bytes 1081344 | tf_op jit(solution)/shard_map/reduce_scatter | solution.py:72
  32.1 12.7 %copy-start.7 = (s32[288]{0:T(512)S(1)}, s32[288]{0:T(512)}, u32[]{:S(2)}) copy-start(s32[288]{0:T(512)} %param.20) | copy-start | bytes 3460
  32.1 12.8 %copy-start.8 = (s32[288]{0:T(512)S(1)}, s32[288]{0:T(512)}, u32[]{:S(2)}) copy-start(s32[288]{0:T(512)} %param.19) | copy-start | bytes 3460
  47.3 2.7 copy-start.4
  130.2 223.9 %copy-start.6 = (f32[128,128]{1,0:T(8,128)S(1)}, f32[128,128]{1,0:T(8,128)}, u32[]{:S(2)}) copy-start(f32[128,128]{1,0:T(8,128)} %param.17) | copy-start | bytes 196612
  356.1 29.3 %all-to-all-start = ((bf16[32,128,128]{2,1,0:T(8,128)(2,1)}), bf16[32,128,128]{2,1,0:T(8,128)(2,1)S(1)}, u32[]{:S(2)}, u32[]{:S(2)}) async-start(bf16[32,128,128]{2,1,0:T(8,128)(2,1)} %stack.4), calls=%async_computation.1 | async-start | bytes 2097152 | tf_op jit(solution)/shard_map/all_to_all | solution.py:14
  362.9 418.1 %reduce-scatter.5.cloned.1.call-start = ((), (), s32[]{:S(2)}) async-start(), calls=%async_computation.5 | async-start | bytes 1081344 | tf_op jit(solution)/shard_map/reduce_scatter | solution.py:72
  473.6 4.5 copy-start
  476.0 2.1 copy-start.2
  479.9 2.7 copy-start.5
  783.2 29.5 %all-to-all-start.1 = ((bf16[32,128,128]{2,1,0:T(8,128)(2,1)}), bf16[32,128,128]{2,1,0:T(8,128)(2,1)S(1)}, u32[]{:S(2)}, u32[]{:S(2)}) async-start(bf16[32,128,128]{2,1,0:T(8,128)(2,1)} %stack.5), calls=%async_computation.3 | async-start | bytes 2097152 | tf_op jit(solution)/shard_map/all_to_all | solution.py:14
  900.9 2.5 copy-start.1
  900.9 3.5 copy-start.3
Sparse Core Ops, SparseCore 0:
  134.1 219.9 reduce-scatter.2
  566.5 214.5 reduce-scatter.4
